TPU v7x, 256 devices: a whole 4x4x8 slice. The times are simulated.
256 devices in a mesh: expert: 32 (over y, x, core), group: 8 (over z).
Axes of the slice: x: 4, y: 4, z: 8, core: 2. Of those that a mesh axis runs over, the one named last changes fastest.
Arguments:
- activations: bfloat16 [4096, 7168], P('expert', 'group'), may hold values from -6 to 6
- out_grads: bfloat16 [4096, 7168], P('expert', 'group'), may hold values from -6 to 6
- sketch_op: bfloat16 [7168, 128], P('group'), may hold values from -0.0625 to 0.0625
- block_lists: int32 [256, 32], P('expert'), may hold values from 0 to 31, as said below
- block_counts: int32 [256], P('expert'), may hold values from 1 to 32
- gate_values: bfloat16 [256, 32, 128], P('expert'), may hold values from 0.05 to 9, as said below
Outputs:
- basis_out: float32 [256, 7168, 128], P('expert', 'group')
Inputs may be any that keep to these rules, and one draw needn't show every extreme that they name: `block_lists`: each row is an ordering of all 32 block numbers, each once. `gate_values`: positive.
All inputs are finite; a program needn't handle non-finite values.
Results may differ from a plain program's by a relative error of at most 0.0042.
The roundings to bfloat16 on the way count: a program that leaves them out, or rounds other values in their place, can miss the bound.
Values may be sent and summed in bfloat16 or wider, within the bound.
No kernel may reach another device: no remote copies, remote signals or barrier semaphores. Data moves between devices by JAX's collectives and lax.ppermute only.
A program may use at most 64 MiB of HBM per device.

v0:
```python
import math
import jax
import jax.numpy as jnp
from jax import lax
from jax.sharding import PartitionSpec as P


def sketch_rows(rows_x, rows_y, weight_part):
    count_exp = weight_part.shape[0]
    row_count = rows_x.shape[0]
    sketch_rank = rows_y.shape[1]
    rows_wide = rows_y.astype(jnp.float32)
    contract = (((0,), (0,)), ((), ()))
    scaled = (weight_part.T[:, :, None] * rows_wide[:, None, :]).astype(jnp.bfloat16)
    scaled = scaled.reshape(row_count, count_exp * sketch_rank)
    return lax.dot_general(rows_x, scaled, contract, preferred_element_type=jnp.float32)


def gram_of(sketch_flat, sketch_rank):
    shaped = sketch_flat.reshape(sketch_flat.shape[0], -1, sketch_rank)
    return jnp.einsum("dkr,dks->rs", shaped, shaped, precision=lax.Precision.HIGHEST)


def on_device(activations, out_grads, sketch_op, block_lists, block_counts, gate_values):
    sketch_rank = sketch_op.shape[1]
    feat_width = activations.shape[1]
    local_exp = block_lists.shape[0]
    blocks = block_lists.shape[1]
    partial_sketch = jnp.dot(out_grads, sketch_op, preferred_element_type=jnp.float32)
    sketched = lax.psum(partial_sketch, "group").astype(jnp.bfloat16)
    slot_ids = jnp.arange(blocks, dtype=jnp.int32)
    slot_live = slot_ids[None, :] < block_counts[:, None]
    onehot = ((block_lists[:, :, None] == slot_ids[None, None, :]) & slot_live[:, :, None]).astype(
        jnp.float32
    )
    weights = jnp.einsum("ejb,ejt->ebt", onehot, gate_values.astype(jnp.float32)).reshape(
        local_exp, -1
    )
    piece_rows = lax.all_gather(activations, "expert", axis=0, tiled=True)
    piece_sketch = lax.all_gather(sketched, "expert", axis=0, tiled=True)
    sketch_all = sketch_rows(piece_rows, piece_sketch, weights)
    gram_total = lax.psum(gram_of(sketch_all, sketch_rank), ("expert", "group"))
    factor = jnp.linalg.cholesky(gram_total)
    stacked = (
        sketch_all.reshape(feat_width, local_exp, sketch_rank)
        .transpose(1, 0, 2)
        .reshape(-1, sketch_rank)
    )
    basis_flat = lax.linalg.triangular_solve(
        factor, stacked, left_side=False, lower=True, transpose_a=True
    )
    out_scale = math.sqrt(local_exp * lax.axis_size("expert") * feat_width * lax.axis_size("group"))
    return (basis_flat * out_scale).reshape(local_exp, feat_width, sketch_rank)


def solution(mesh):
    in_specs = (
        P("expert", "group"),
        P("expert", "group"),
        P("group", None),
        P("expert", None),
        P("expert"),
        P("expert", None, None),
    )
    out_specs = P("expert", "group", None)
    return jax.shard_map(
        on_device, mesh=mesh, in_specs=in_specs, out_specs=out_specs, check_vma=False
    )
```

profile of v0, /device:TPU:1, one launch (start us, length us, event | category | flops | bytes accessed | tf_op | source)
XLA Modules:
  0.0 443.5 jit_solution(5734964180359648877)
XLA Ops:
  6.5 0.0 copy-start
  6.5 0.0 all-gather.3.cloned.1.call-start
  6.5 0.9 copy-done
  7.5 1.1 fusion.10
  8.6 27.5 %psum.14 = bf16[128,128]{1,0:T(8,128)(2,1)} all-reduce(f32[128,128]{1,0:T(8,128)S(1)} %fusion.10), channel_id=1, replica_groups=mesh['expert'=32,'group'=8] {'group'}, use_global_device_ids=true, to_apply=%region_0.0 | all-reduce | flops 16384 | bytes 98304 | tf_op jit(solution)/shard_map/psum | solution.py:30
  36.2 0.0 all-gather.3.cloned.1.call-update
  36.2 0.0 all-gather.5.cloned.1.call-start
  36.2 0.7 all-gather.5.cloned.1.call-update
  36.9 0.0 all-reduce.2.cloned.1.call-start
  37.0 0.7 iota_compare_fusion.3
  37.7 1.0 convolution_bitcast_fusion
  38.7 0.1 copy.26
  38.8 0.6 copy.11
  39.4 50.1 %all-gather.3.cloned.1.call-done = bf16[4096,128]{1,0:T(8,128)(2,1)} async-done(((bf16[128,128]{1,0:T(8,128)(2,1)}), bf16[4096,128]{1,0:T(8,128)(2,1)}) %all-gather.3.cloned.1.call-update) | async-done | bytes 1048592 | tf_op jit(solution)/shard_map/all_gather | solution.py:40
  89.5 1.4 convert_element_type.16
  90.9 16.4 %multiply_convert_fusion = bf16[4096,8,128]{2,1,0:T(8,128)(2,1)} fusion(f32[4096,128]{1,0:T(8,128)S(1)} %convert_element_type.16, f32[4096,8]{1,0:T(8,128)S(1)} %copy.11), kind=kLoop, calls=%fused_computation | loop fusion | flops 8388608 | bytes 10616832 | tf_op jit(solution)/shard_map/convert_element_type | solution.py:14
  107.2 40.0 %all-gather.5.cloned.1.call-done = bf16[4096,896]{1,0:T(8,128)(2,1)} async-done(((bf16[128,896]{1,0:T(8,128)(2,1)}), bf16[4096,896]{1,0:T(8,128)(2,1)}) %all-gather.5.cloned.1.call-update) | async-done | bytes 7340048 | tf_op jit(solution)/shard_map/all_gather | solution.py:39
  147.3 12.9 %fusion = f32[1024,896]{1,0:T(8,128)S(1)} fusion(bf16[4096,896]{1,0:T(8,128)(2,1)} %all-gather.5.cloned.1.call-done, bf16[512,8,8,128]{3,2,1,0:T(8,128)(2,1)} %bitcast.40), kind=kOutput, calls=%fused_computation.2 | convolution fusion | flops 7516192768 | bytes 19398656 | tf_op jit(solution)/shard_map/dot_general | solution.py:16
  160.2 0.0 copy-start.1
  160.2 1.8 copy-done.1
  162.1 3.6 convolution_bitcast_fusion.1
  165.7 0.0 all-reduce.2.cloned.1.call-update
  165.7 5.0 %copy.12 = f32[896,8,128]{2,0,1:T(8,128)} copy(f32[896,8,128]{0,2,1:T(8,128)} %bitcast.38) | data formatting | bytes 7340032 | tf_op jit(solution)/shard_map/reshape | solution.py:45
  170.7 235.7 %all-reduce.2.cloned.1.call-done = f32[128,128]{0,1:T(8,128)} async-done(((f32[128,128]{0,1:T(8,128)}), f32[128,128]{0,1:T(8,128)}) %all-reduce.2.cloned.1.call-update) | async-done | bytes 65552 | tf_op jit(solution)/shard_map/psum | solution.py:42
  406.4 0.9 copy.15
  407.4 0.9 fusion.7
  408.2 11.7 %cholesky.16 = f32[128,128]{1,0:T(8,128)S(1)} custom-call(f32[128,128]{1,0:T(8,128)S(1)} %fusion.7), custom_call_target="Cholesky" | custom-call | tf_op jit(solution)/shard_map/jit(cholesky)/cholesky | solution.py:43
  420.0 0.6 compare_reduce_fusion
  420.6 0.7 fusion.5
  421.3 9.8 %custom-call.6 = f32[1,128,128]{1,2,0:T(8,128)S(1)} custom-call(f32[1,128,128]{2,1,0:T(8,128)S(1)} %fusion.5), custom_call_target="InvertDiagBlocksLowerTriangular" | custom-call | tf_op jit(solution)/shard_map/triangular_solve | solution.py:49
  431.1 5.9 %convolution_multiply_fusion = f32[7168,128]{1,0:T(8,128)} fusion(f32[7168,128]{1,0:T(8,128)} %bitcast.39, f32[1,128,128]{1,2,0:T(8,128)S(1)} %custom-call.6), kind=kOutput, calls=%fused_computation.1 | convolution fusion | flops 1410203648 | bytes 7405568 | tf_op jit(solution)/shard_map/triangular_solve | solution.py:49
  (1 shorter events, 0.0 us)
Async XLA Ops:
  6.5 0.9 copy-start
  6.5 83.0 %all-gather.3.cloned.1.call-start = ((), (), s32[]{:S(2)}) async-start(), calls=%async_computation | async-start | bytes 1081344 | tf_op jit(solution)/shard_map/all_gather | solution.py:40
  36.2 111.1 %all-gather.5.cloned.1.call-start = ((), (), s32[]{:S(2)}) async-start(), calls=%async_computation.1 | async-start | bytes 7569408 | tf_op jit(solution)/shard_map/all_gather | solution.py:39
  36.9 369.5 %all-reduce.2.cloned.1.call-start = ((), (), s32[]{:S(2)}) async-start(), calls=%async_computation.2 | async-start | bytes 131072 | tf_op jit(solution)/shard_map/psum | solution.py:42
  160.2 1.8 copy-start.1
Sparse Core Ops, SparseCore 0:
  36.3 53.1 all-gather.2
  92.0 55.1 all-gather.4
  165.8 240.5 all-reduce.1
where the time goes:
time: 444 us
  waiting for transfers between devices  327 us (74%)
  other arithmetic  42.2 us (10%)
  blocking collectives  27.5 us (6%)
  matrix products  24.7 us (6%)
  between operations  13.2 us (3%)
  local copies, waits for them, and re-layouts  9.39 us (2%)
    psum x1, waiting for transfers between devices, on_device(): gram_total = lax.psum(gram_of(sketch_all, sketch_rank), ('expert', 'group'))  236 us
    all_gather x1, waiting for transfers between devices, on_device(): piece_sketch = lax.all_gather(sketched, 'expert', axis=0, tiled=True)  50.1 us
    all_gather x1, waiting for transfers between devices, on_device(): piece_rows = lax.all_gather(activations, 'expert', axis=0, tiled=True)  40 us
    psum x1, blocking collectives, on_device(): sketched = lax.psum(partial_sketch, 'group').astype(jnp.bfloat16)  27.5 us
    convert_element_type x1, other arithmetic, sketch_rows(): (weight_part.T[:, :, None] * rows_wide[:, None, :]).astype(jnp.bfloat16)  16.4 us
    dot_general x1, matrix products, sketch_rows(): lax.dot_general(rows_x, scaled, contract, preferred_element_type=jnp.floa...  12.9 us
    another operation x3, other arithmetic, on_device(): factor = jnp.linalg.cholesky(gram_total)  12.4 us
    another operation x2, other arithmetic, on_device(): lax.linalg.triangular_solve(factor, stacked, left_side=False, lower=True,...  10.5 us
  transfers between devices with their start and end apart: 3, of which 3 were waited for; matrix products, arithmetic and copies ran while one was open for 6% of the time, Pallas kernels for 0%

commit v1 on v0

--- a/solution.py
+++ b/solution.py
@@ -39,7 +39,7 @@
     piece_rows = lax.all_gather(activations, "expert", axis=0, tiled=True)
     piece_sketch = lax.all_gather(sketched, "expert", axis=0, tiled=True)
     sketch_all = sketch_rows(piece_rows, piece_sketch, weights)
-    gram_total = lax.psum(gram_of(sketch_all, sketch_rank), ("expert", "group"))
+    gram_total = lax.psum(lax.psum(gram_of(sketch_all, sketch_rank), "expert"), "group")
     factor = jnp.linalg.cholesky(gram_total)
     stacked = (
         sketch_all.reshape(feat_width, local_exp, sketch_rank)

time: 444 us -> 382 us (0.86)
  waiting for transfers between devices: 327 us -> 260 us
    psum x1 -> x2, waiting for transfers between devices: 236 us -> 170 us  [the longest x1 106 us: on_device(): lax.psum(gram_of(sketch_all, sketch_rank), 'expert')]
  transfers between devices with their start and end apart: 3 -> 4, of which waited for: 3 -> 4; matrix products, arithmetic and copies ran while one was open for 6% -> 7% of each run, Pallas kernels for 0% -> 0%
where the time goes in v1:
time: 382 us; the launch traced here: 378 us
  waiting for transfers between devices  260 us (68%)
  other arithmetic  42.2 us (11%)
  blocking collectives  27.5 us (7%)
  matrix products  24.7 us (6%)
  between operations  13.2 us (3%)
  local copies, waits for them, and re-layouts  9.39 us (2%)
    psum x1, waiting for transfers between devices, on_device(): lax.psum(gram_of(sketch_all, sketch_rank), 'expert')  106 us
    psum x1, waiting for transfers between devices, on_device(): lax.psum(lax.psum(gram_of(sketch_all, sketch_rank), 'expert'), 'group')  63.2 us
    all_gather x1, waiting for transfers between devices, on_device(): piece_sketch = lax.all_gather(sketched, 'expert', axis=0, tiled=True)  50.1 us
    all_gather x1, waiting for transfers between devices, on_device(): piece_rows = lax.all_gather(activations, 'expert', axis=0, tiled=True)  40 us
    psum x1, blocking collectives, on_device(): sketched = lax.psum(partial_sketch, 'group').astype(jnp.bfloat16)  27.5 us
    convert_element_type x1, other arithmetic, sketch_rows(): (weight_part.T[:, :, None] * rows_wide[:, None, :]).astype(jnp.bfloat16)  16.4 us
    dot_general x1, matrix products, sketch_rows(): lax.dot_general(rows_x, scaled, contract, preferred_element_type=jnp.floa...  12.9 us
    another operation x3, other arithmetic, on_device(): factor = jnp.linalg.cholesky(gram_total)  12.4 us
  transfers between devices with their start and end apart: 4, of which 4 were waited for; matrix products, arithmetic and copies ran while one was open for 7% of the time, Pallas kernels for 0%

profile of v1, /device:TPU:1, one launch (start us, length us, event | category | flops | bytes accessed | tf_op | source)
XLA Modules:
  0.0 377.7 jit_solution(11500558794340875962)
XLA Ops:
  6.5 0.0 copy-start
  6.5 0.0 all-gather.3.cloned.1.call-start
  6.5 0.9 copy-done
  7.5 1.1 fusion.10
  8.6 27.5 %psum.21 = bf16[128,128]{1,0:T(8,128)(2,1)} all-reduce(f32[128,128]{1,0:T(8,128)S(1)} %fusion.10), channel_id=1, replica_groups=mesh['expert'=32,'group'=8] {'group'}, use_global_device_ids=true, to_apply=%region_0.0 | all-reduce | flops 16384 | bytes 98304 | tf_op jit(solution)/shard_map/psum | solution.py:30
  36.2 0.0 all-gather.3.cloned.1.call-update
  36.2 0.0 all-gather.5.cloned.1.call-start
  36.2 0.7 all-gather.5.cloned.1.call-update
  36.9 0.0 all-reduce.3.cloned.1.call-start
  37.0 0.7 iota_compare_fusion.3
  37.7 1.0 convolution_bitcast_fusion
  38.7 0.1 copy.26
  38.8 0.6 copy.11
  39.4 50.1 %all-gather.3.cloned.1.call-done = bf16[4096,128]{1,0:T(8,128)(2,1)} async-done(((bf16[128,128]{1,0:T(8,128)(2,1)}), bf16[4096,128]{1,0:T(8,128)(2,1)}) %all-gather.3.cloned.1.call-update) | async-done | bytes 1048592 | tf_op jit(solution)/shard_map/all_gather | solution.py:40
  89.5 1.4 convert_element_type.16
  90.9 16.4 %multiply_convert_fusion = bf16[4096,8,128]{2,1,0:T(8,128)(2,1)} fusion(f32[4096,128]{1,0:T(8,128)S(1)} %convert_element_type.16, f32[4096,8]{1,0:T(8,128)S(1)} %copy.11), kind=kLoop, calls=%fused_computation | loop fusion | flops 8388608 | bytes 10616832 | tf_op jit(solution)/shard_map/convert_element_type | solution.py:14
  107.2 40.0 %all-gather.5.cloned.1.call-done = bf16[4096,896]{1,0:T(8,128)(2,1)} async-done(((bf16[128,896]{1,0:T(8,128)(2,1)}), bf16[4096,896]{1,0:T(8,128)(2,1)}) %all-gather.5.cloned.1.call-update) | async-done | bytes 7340048 | tf_op jit(solution)/shard_map/all_gather | solution.py:39
  147.3 12.9 %fusion = f32[1024,896]{1,0:T(8,128)S(1)} fusion(bf16[4096,896]{1,0:T(8,128)(2,1)} %all-gather.5.cloned.1.call-done, bf16[512,8,8,128]{3,2,1,0:T(8,128)(2,1)} %bitcast.40), kind=kOutput, calls=%fused_computation.2 | convolution fusion | flops 7516192768 | bytes 19398656 | tf_op jit(solution)/shard_map/dot_general | solution.py:16
  160.2 0.0 copy-start.1
  160.2 1.8 copy-done.1
  162.1 3.6 convolution_bitcast_fusion.1
  165.7 0.0 all-reduce.3.cloned.1.call-update
  165.7 0.2 all-reduce.5.cloned.1.call-start
  166.0 106.4 %all-reduce.3.cloned.1.call-done = f32[128,128]{0,1:T(8,128)} async-done(((f32[128,128]{0,1:T(8,128)}), f32[128,128]{0,1:T(8,128)}) %all-reduce.3.cloned.1.call-update) | async-done | bytes 65552 | tf_op jit(solution)/shard_map/psum | solution.py:42
  272.3 0.0 all-reduce.5.cloned.1.call-update
  272.4 5.0 %copy.12 = f32[896,8,128]{2,0,1:T(8,128)} copy(f32[896,8,128]{0,2,1:T(8,128)} %bitcast.38) | data formatting | bytes 7340032 | tf_op jit(solution)/shard_map/reshape | solution.py:45
  277.4 63.2 %all-reduce.5.cloned.1.call-done = f32[128,128]{0,1:T(8,128)} async-done(((f32[128,128]{0,1:T(8,128)}), f32[128,128]{0,1:T(8,128)}) %all-reduce.5.cloned.1.call-update) | async-done | bytes 65552 | tf_op jit(solution)/shard_map/psum | solution.py:42
  340.6 0.9 copy.15
  341.5 0.9 fusion.7
  342.3 11.7 %cholesky.16 = f32[128,128]{1,0:T(8,128)S(1)} custom-call(f32[128,128]{1,0:T(8,128)S(1)} %fusion.7), custom_call_target="Cholesky" | custom-call | tf_op jit(solution)/shard_map/jit(cholesky)/cholesky | solution.py:43
  354.1 0.6 compare_reduce_fusion
  354.7 0.7 fusion.5
  355.4 9.8 %custom-call.6 = f32[1,128,128]{1,2,0:T(8,128)S(1)} custom-call(f32[1,128,128]{2,1,0:T(8,128)S(1)} %fusion.5), custom_call_target="InvertDiagBlocksLowerTriangular" | custom-call | tf_op jit(solution)/shard_map/triangular_solve | solution.py:49
  365.2 5.9 %convolution_multiply_fusion = f32[7168,128]{1,0:T(8,128)} fusion(f32[7168,128]{1,0:T(8,128)} %bitcast.39, f32[1,128,128]{1,2,0:T(8,128)S(1)} %custom-call.6), kind=kOutput, calls=%fused_computation.1 | convolution fusion | flops 1410203648 | bytes 7405568 | tf_op jit(solution)/shard_map/triangular_solve | solution.py:49
  (1 shorter events, 0.0 us)
Async XLA Ops:
  6.5 0.9 copy-start
  6.5 83.0 %all-gather.3.cloned.1.call-start = ((), (), s32[]{:S(2)}) async-start(), calls=%async_computation | async-start | bytes 1081344 | tf_op jit(solution)/shard_map/all_gather | solution.py:40
  36.2 111.1 %all-gather.5.cloned.1.call-start = ((), (), s32[]{:S(2)}) async-start(), calls=%async_computation.1 | async-start | bytes 7569408 | tf_op jit(solution)/shard_map/all_gather | solution.py:39
  36.9 235.4 %all-reduce.3.cloned.1.call-start = ((), (), s32[]{:S(2)}) async-start(), calls=%async_computation.2 | async-start | bytes 131072 | tf_op jit(solution)/shard_map/psum | solution.py:42
  160.2 1.8 copy-start.1
  165.7 174.8 %all-reduce.5.cloned.1.call-start = ((), (), s32[]{:S(2)}) async-start(), calls=%async_computation.3 | async-start | bytes 131072 | tf_op jit(solution)/shard_map/psum | solution.py:42
Sparse Core Ops, SparseCore 0:
  36.3 53.1 all-gather.2
  92.0 55.1 all-gather.4
  165.8 106.4 all-reduce.2
  274.5 66.0 all-reduce.4
